TPU v7x, 32 devices: a whole 2x2x4 slice. The times are simulated.
32 devices in a mesh: dp: 8 (over y, x, core), mp: 4 (over z).
Axes of the slice: x: 2, y: 2, z: 4, core: 2. Of those that a mesh axis runs over, the one named last changes fastest.
Arguments:
- inputs: bfloat16 [8, 3072, 768], P('dp'), may hold values from -6 to 6
- counts: int32 [8], P('dp'), may hold values from 1024 to 3072, as said below
- first_gain: float32 [768], replicated, may hold values from 0.5 to 1.5
- first_bias: float32 [768], replicated, may hold values from -4 to 4
- query_key_value_weight: bfloat16 [768, 3, 768], P(None, None, 'mp'), may hold values from -0.21875 to 0.21875
- query_bias: float32 [768], P('mp'), may hold values from -6 to 6
- value_bias: float32 [768], P('mp'), may hold values from -0.75 to 0.75
- w_out: bfloat16 [768, 768], P('mp'), may hold values from -4 to 4
- out_bias: float32 [768], replicated, may hold values from -4 to 4
- second_gain: float32 [768], replicated, may hold values from 0.5 to 1.5
- second_bias: float32 [768], replicated, may hold values from -4 to 4
- w_up: bfloat16 [768, 3072], P(None, 'mp'), may hold values from -0.21875 to 0.21875
- up_bias: float32 [3072], P('mp'), may hold values from -4 to 4
- w_down: bfloat16 [3072, 768], P('mp'), may hold values from -0.109375 to 0.109375
- down_bias: float32 [768], replicated, may hold values from -4 to 4
- out_grad: bfloat16 [8, 3072, 768], P('dp'), may hold values from -6 to 6
Outputs:
- outputs: bfloat16 [8, 3072, 768], P('dp')
- input_grad: float32 [8, 3072, 768], P('dp')
- grad_first_gain: float32 [768], replicated
- grad_first_bias: float32 [768], replicated
- query_key_value_gradient: float32 [768, 3, 768], P(None, None, 'mp')
- grad_query_bias: float32 [768], P('mp')
- grad_value_bias: float32 [768], P('mp')
- grad_out: float32 [768, 768], P('mp')
- grad_out_bias: float32 [768], replicated
- grad_second_gain: float32 [768], replicated
- grad_second_bias: float32 [768], replicated
- grad_up: float32 [768, 3072], P(None, 'mp')
- grad_up_bias: float32 [3072], P('mp')
- grad_down: float32 [3072, 768], P('mp')
- grad_down_bias: float32 [768], replicated
Inputs may be any that keep to these rules, and one draw needn't show every extreme that they name: `counts`: each cell's count lies between 1024 and 3072; the first cell has exactly 3072 genes.
All inputs are finite; a program needn't handle non-finite values.
Results may differ from a plain program's by a relative error of at most 0.012.
The roundings to bfloat16 on the way count: a program that leaves them out, or rounds other values in their place, can miss the bound.
Values may be sent and summed in bfloat16 or wider, within the bound.
A program may use at most 192 MiB of HBM per device.

v0:
```python
from functools import partial

import jax
import jax.numpy as jnp
from jax import lax
from jax.sharding import PartitionSpec as P

HEAD_DIM = 64
QB = 512


def row_stats(row_block):
    centred = row_block - jnp.mean(row_block, axis=-1, keepdims=True)
    inverse = lax.rsqrt(jnp.mean(centred * centred, axis=-1, keepdims=True) + 1e-05)
    return (centred * inverse, inverse)


def norm_back(grad_norm, normed, inverse, scales):
    scaled = grad_norm * scales
    grad_rows = inverse * (
        scaled
        - jnp.mean(scaled, axis=-1, keepdims=True)
        - normed * jnp.mean(scaled * normed, axis=-1, keepdims=True)
    )
    return (grad_rows, jnp.sum(grad_norm * normed, axis=0), jnp.sum(grad_norm, axis=0))


def block_scores(query_block, key_rows, keymask, score_scale):
    scores = (
        jnp.einsum("qhd,khd->hqk", query_block, key_rows, preferred_element_type=jnp.float32)
        * score_scale
    )
    return jnp.where(keymask[None, None, :], scores, -1e30)


def cell_forward(queries, key_rows, value_rows, length, score_scale):
    keymask = jnp.arange(key_rows.shape[0]) < length

    def one_block(block_index):
        query_block = lax.dynamic_slice_in_dim(queries, block_index * QB, QB, 0)
        scores = block_scores(query_block, key_rows, keymask, score_scale)
        maxima = jnp.max(scores, axis=-1, keepdims=True)
        powers = jnp.exp(scores - maxima)
        totals = jnp.sum(powers, axis=-1, keepdims=True)
        weights = (powers / totals).astype(jnp.bfloat16)
        context = jnp.einsum(
            "hqk,khd->qhd", weights, value_rows, preferred_element_type=jnp.float32
        )
        return (context.astype(jnp.bfloat16), (maxima + jnp.log(totals))[..., 0])

    return lax.map(one_block, jnp.arange(key_rows.shape[0] // QB))


def cell_backward(queries, key_rows, value_rows, grad_context, log_totals, length, score_scale):
    keymask = jnp.arange(key_rows.shape[0]) < length

    def compute(block_index):
        query_block = lax.dynamic_slice_in_dim(queries, block_index * QB, QB, 0)
        grad_block = lax.dynamic_slice_in_dim(grad_context, block_index * QB, QB, 0)
        block_totals = lax.dynamic_index_in_dim(log_totals, block_index, 0, keepdims=False)
        scores = block_scores(query_block, key_rows, keymask, score_scale)
        weights = jnp.exp(scores - block_totals[..., None])
        weights_low = weights.astype(jnp.bfloat16)
        grad_weights = jnp.einsum(
            "qhd,khd->hqk", grad_block, value_rows, preferred_element_type=jnp.float32
        )
        row_dot = jnp.sum(grad_weights * weights, axis=-1, keepdims=True)
        grad_scores = (weights * (grad_weights - row_dot)).astype(jnp.bfloat16)
        grad_queries = (
            jnp.einsum("hqk,khd->qhd", grad_scores, key_rows, preferred_element_type=jnp.float32)
            * score_scale
        )
        key_term = (
            jnp.einsum("hqk,qhd->khd", grad_scores, query_block, preferred_element_type=jnp.float32)
            * score_scale
        )
        value_term = jnp.einsum(
            "hqk,qhd->khd", weights_low, grad_block, preferred_element_type=jnp.float32
        )
        return (grad_queries, key_term, value_term)

    def one_block(carry, block_index):
        grad_queries, key_term, value_term = compute(block_index)
        return ((carry[0] + key_term, carry[1] + value_term), grad_queries)

    start_keys = jnp.zeros(key_rows.shape, jnp.float32)
    (grad_keys, grad_values), grad_queries = lax.scan(
        one_block, (start_keys, start_keys), jnp.arange(key_rows.shape[0] // QB)
    )
    return (grad_queries, grad_keys, grad_values)


def per_device(
    inputs,
    counts,
    first_gain,
    first_bias,
    query_key_value_weight,
    query_bias,
    value_bias,
    w_out,
    out_bias,
    second_gain,
    second_bias,
    w_up,
    up_bias,
    w_down,
    down_bias,
    out_grad,
):
    cell_count, slot_count, features = inputs.shape
    row_count = cell_count * slot_count
    local_width = query_key_value_weight.shape[2]
    head_count = local_width // HEAD_DIM
    share_rows = row_count // lax.axis_size("mp")
    first_row = lax.axis_index("mp") * share_rows
    score_scale = HEAD_DIM ** (-0.5)
    flattened = inputs.reshape(row_count, features).astype(jnp.float32)
    valid = (
        (jnp.arange(slot_count)[None, :] < counts[:, None])
        .astype(jnp.float32)
        .reshape(row_count, 1)
    )
    normed_one, inverse_one = row_stats(flattened)
    first_norm_input = (normed_one * first_gain + first_bias).astype(jnp.bfloat16)
    projected_rows = jnp.einsum(
        "yc,cur->uyr", first_norm_input, query_key_value_weight, preferred_element_type=jnp.float32
    )
    head_shape = (cell_count, slot_count, head_count, HEAD_DIM)
    queries = (projected_rows[0] + query_bias).astype(jnp.bfloat16).reshape(head_shape)
    key_rows = projected_rows[1].astype(jnp.bfloat16).reshape(head_shape)
    value_rows = (projected_rows[2] + value_bias).astype(jnp.bfloat16).reshape(head_shape)
    context, log_totals = lax.map(
        lambda items: cell_forward(items[0], items[1], items[2], items[3], score_scale),
        (queries, key_rows, value_rows, counts),
    )
    context = context.reshape(row_count, local_width)
    inputs_share = lax.dynamic_slice_in_dim(flattened, first_row, share_rows, 0)
    segment_ids = context
    mixed_share = (
        inputs_share
        + lax.psum_scatter(
            jnp.dot(segment_ids, w_out, preferred_element_type=jnp.float32),
            "mp",
            scatter_dimension=0,
            tiled=True,
        )
        + out_bias
    )
    normed_two, inverse_two = row_stats(mixed_share)
    second_share = (normed_two * second_gain + second_bias).astype(jnp.bfloat16)
    segment_ids = lax.all_gather(second_share, "mp", axis=0, tiled=True)
    second_in = segment_ids
    up_input = jnp.dot(segment_ids, w_up, preferred_element_type=jnp.float32) + up_bias
    activated = jax.nn.gelu(up_input, approximate=False).astype(jnp.bfloat16)
    segment_ids = activated
    out_share = (
        mixed_share
        + lax.psum_scatter(
            jnp.dot(segment_ids, w_down, preferred_element_type=jnp.float32).astype(jnp.bfloat16),
            "mp",
            scatter_dimension=0,
            tiled=True,
        ).astype(jnp.float32)
        + down_bias
    ).astype(jnp.bfloat16)
    outputs = lax.all_gather(out_share, "mp", axis=0, tiled=True).reshape(
        cell_count, slot_count, features
    )
    grad_y = out_grad.reshape(row_count, features).astype(jnp.float32) * valid
    grad_low = grad_y.astype(jnp.bfloat16)
    grad_down = jnp.einsum("tf,td->fd", activated, grad_low, preferred_element_type=jnp.float32)
    grad_down_bias = jnp.sum(grad_low, axis=0, dtype=jnp.float32)
    grad_act = jnp.einsum("td,fd->tf", grad_low, w_down, preferred_element_type=jnp.float32)
    unused, gelu_back = jax.vjp(partial(jax.nn.gelu, approximate=False), up_input)
    grad_up_low = gelu_back(grad_act)[0].astype(jnp.bfloat16)
    grad_up = jnp.einsum("td,tf->df", second_in, grad_up_low, preferred_element_type=jnp.float32)
    grad_up_bias = jnp.sum(grad_up_low, axis=0, dtype=jnp.float32)
    segment_ids = grad_up_low
    grad_second = lax.psum_scatter(
        jnp.einsum("tf,df->td", segment_ids, w_up, preferred_element_type=jnp.float32),
        "mp",
        scatter_dimension=0,
        tiled=True,
    )
    grad_mixed, grad_second_gain, grad_second_bias = norm_back(
        grad_second, normed_two, inverse_two, second_gain
    )
    grad_mixed = grad_mixed + lax.dynamic_slice_in_dim(grad_y, first_row, share_rows, 0)
    segment_ids = lax.all_gather(grad_mixed.astype(jnp.bfloat16), "mp", axis=0, tiled=True)
    grad_mixed_low = segment_ids
    grad_context = jnp.einsum(
        "td,ed->te", segment_ids, w_out, preferred_element_type=jnp.float32
    ).astype(jnp.bfloat16)
    grad_out = jnp.einsum("te,td->ed", context, grad_mixed_low, preferred_element_type=jnp.float32)
    grad_out_bias = jnp.sum(grad_mixed_low, axis=0, dtype=jnp.float32)
    grad_queries, grad_keys, grad_values = lax.map(
        lambda items: cell_backward(
            items[0], items[1], items[2], items[3], items[4], items[5], score_scale
        ),
        (queries, key_rows, value_rows, grad_context.reshape(head_shape), log_totals, counts),
    )
    stacked_parts = jnp.stack(
        [
            grad_queries.reshape(row_count, local_width).astype(jnp.bfloat16),
            grad_keys.reshape(row_count, local_width).astype(jnp.bfloat16),
            grad_values.reshape(row_count, local_width).astype(jnp.bfloat16),
        ]
    )
    query_key_value_gradient = jnp.einsum(
        "rc,zrn->czn", first_norm_input, stacked_parts, preferred_element_type=jnp.float32
    )
    grad_query_bias = jnp.sum(stacked_parts[0], axis=0, dtype=jnp.float32)
    grad_value_bias = jnp.sum(stacked_parts[2], axis=0, dtype=jnp.float32)
    segment_ids = stacked_parts
    grad_first = lax.psum_scatter(
        jnp.einsum(
            "ocg,yog->cy", segment_ids, query_key_value_weight, preferred_element_type=jnp.float32
        ),
        "mp",
        scatter_dimension=0,
        tiled=True,
    )
    grad_input, grad_first_gain, grad_first_bias = norm_back(
        grad_first,
        lax.dynamic_slice_in_dim(normed_one, first_row, share_rows, 0),
        lax.dynamic_slice_in_dim(inverse_one, first_row, share_rows, 0),
        first_gain,
    )
    grad_input = grad_input + grad_mixed
    input_grad = lax.all_gather(grad_input, "mp", axis=0, tiled=True).reshape(
        cell_count, slot_count, features
    )
    norm_sums = lax.psum(
        (grad_first_gain, grad_first_bias, grad_second_gain, grad_second_bias), ("dp", "mp")
    )
    members = [
        query_key_value_gradient,
        grad_query_bias,
        grad_value_bias,
        grad_out,
        grad_out_bias,
        grad_up,
        grad_up_bias,
        grad_down,
        grad_down_bias,
    ]
    flattened_grads = jnp.concatenate([member.reshape(-1) for member in members])
    summed = lax.psum(flattened_grads, "dp")
    unpacked = []
    position = 0
    for member in members:
        unpacked.append(summed[position : position + member.size].reshape(member.shape))
        position = position + member.size
    return (
        outputs,
        input_grad,
        norm_sums[0],
        norm_sums[1],
        unpacked[0],
        unpacked[1],
        unpacked[2],
        unpacked[3],
        unpacked[4],
        norm_sums[2],
        norm_sums[3],
        unpacked[5],
        unpacked[6],
        unpacked[7],
        unpacked[8],
    )


def solution(mesh):
    return jax.shard_map(
        per_device,
        mesh=mesh,
        in_specs=(
            P("dp", None, None),
            P("dp"),
            P(),
            P(),
            P(None, None, "mp"),
            P("mp"),
            P("mp"),
            P("mp", None),
            P(),
            P(),
            P(),
            P(None, "mp"),
            P("mp"),
            P("mp", None),
            P(),
            P("dp", None, None),
        ),
        out_specs=(
            P("dp", None, None),
            P("dp", None, None),
            P(),
            P(),
            P(None, None, "mp"),
            P("mp"),
            P("mp"),
            P("mp", None),
            P(),
            P(),
            P(),
            P(None, "mp"),
            P("mp"),
            P("mp", None),
            P(),
        ),
        check_vma=False,
    )
```

profile of v0, /device:TPU:0, one launch (start us, length us, event | category | flops | bytes accessed | tf_op | source)
XLA Modules:
  0.0 1786.4 jit_solution(11802532279113605774)
XLA Ops:
  24.0 202.3 %while.48 = (s32[]{:T(128)}, bf16[6,512,3,64]{1,3,2,0:T(8,128)(2,1)}, f32[6,3,512]{2,1,0:T(4,128)}, s32[6]{0:T(128)S(1)}, bf16[3072,3,64]{0,2,1:T(8,128)(2,1)}, ...) while((s32[]{:T(128)}, ...), condition=%wide.region_5.6_spmd.clone, body=%wide.region_2.5_spmd.clone.sunk | while | flops 1264682496 | bytes 59465956 | solution.py:51
  46.0 11.3 fusion.120
  79.7 11.3 fusion.120
  113.3 11.3 fusion.120
  147.0 11.3 fusion.120
  180.7 11.3 fusion.120
  214.4 11.3 fusion.120
  243.1 156.9 %reduce-scatter.5.cloned.1.call-done = f32[768,768]{1,0:T(8,128)} async-done(((f32[3072,768]{1,0:T(8,128)}), f32[768,768]{1,0:T(8,128)}) %reduce-scatter.5.cloned.1.call-update) | async-done | bytes 2359312 | tf_op jit(solution)/shard_map/reduce_scatter | solution.py:142
  405.9 89.2 %all-gather.5.cloned.1.call-done = bf16[3072,768]{1,0:T(8,128)(2,1)} async-done(((bf16[768,768]{1,0:T(8,128)(2,1)}), bf16[3072,768]{1,0:T(8,128)(2,1)}) %all-gather.5.cloned.1.call-update) | async-done | bytes 4718608 | tf_op jit(solution)/shard_map/all_gather | solution.py:152
  495.1 26.5 %multiply_convert_fusion.1 = (bf16[3072,768]{1,0:T(8,128)(2,1)}, f32[3072,768]{1,0:T(8,128)}, f32[3072,768]{1,0:T(8,128)}) fusion(f32[768]{0:T(1024)} %param.32, bf16[3072,768]{1,0:T(8,128)(2,1)} %all-gather.5.cloned.1.call-done, bf16[768,768]{1,0:T(8,128)(2,1)S(1)} %copy-done), kind=kOutput, calls=%fused_computation.54 | convolution fusion | flops 3779592192 | bytes 29494272 | tf_op jit(solution)/shard_map/dot_general | solution.py:154
  521.6 12.8 convert_reduce_fusion.1
  560.2 142.3 %reduce-scatter.9.cloned.1.call-done = f32[768,768]{1,0:T(8,128)} async-done(((f32[3072,768]{1,0:T(8,128)}), f32[768,768]{1,0:T(8,128)}) %reduce-scatter.9.cloned.1.call-update) | async-done | bytes 2359312 | tf_op jit(solution)/shard_map/reduce_scatter | solution.py:180
  705.8 85.2 %reduce-scatter.7.cloned.1.call-done = bf16[768,768]{1,0:T(8,128)(2,1)} async-done(((bf16[3072,768]{1,0:T(8,128)(2,1)}), bf16[768,768]{1,0:T(8,128)(2,1)}) %reduce-scatter.7.cloned.1.call-update) | async-done | bytes 1179664 | tf_op jit(solution)/shard_map/reduce_scatter | solution.py:159
  820.6 65.1 %all-gather.9.cloned.1.call-done = bf16[3072,768]{1,0:T(8,128)(2,1)} async-done(((bf16[768,768]{1,0:T(8,128)(2,1)}), bf16[3072,768]{1,0:T(8,128)(2,1)}) %all-gather.9.cloned.1.call-update) | async-done | bytes 4718608 | tf_op jit(solution)/shard_map/all_gather | solution.py:190
  890.8 333.3 %while.49 = (s32[]{:T(128)}, f32[3072,3,64]{0,2,1:T(8,128)S(1)}, f32[3072,3,64]{0,2,1:T(8,128)}, bf16[6,512,3,64]{1,3,2,0:T(8,128)(2,1)}, s32[6]{0:T(128)S(1)}, ...) while((s32[]{:T(128)}, f32[3072,3,64]{0,2,1:T(8,128)S(1)}, ...), condition=%wide.region_15.16_spmd.clone, body=%wide.region_13.15_spmd.clone.sunk | while | flops 3093726720 | bytes 231266608 | solution.py:87
  912.4 13.4 multiply_reduce_fusion.10
  925.8 13.7 multiply_convert_fusion.3
  968.2 13.3 multiply_reduce_fusion.10
  981.4 13.6 multiply_convert_fusion.3
  1023.7 13.3 multiply_reduce_fusion.10
  1037.0 13.6 multiply_convert_fusion.3
  1079.3 13.3 multiply_reduce_fusion.10
  1092.5 13.6 multiply_convert_fusion.3
  1134.8 13.3 multiply_reduce_fusion.10
  1148.1 13.6 multiply_convert_fusion.3
  1190.4 13.3 multiply_reduce_fusion.10
  1203.6 13.6 multiply_convert_fusion.3
  1257.7 59.5 %concatenate.3 = f32[1772160]{0:T(1024)} concatenate(f32[442368]{0:T(1024)} %reshape.244, f32[192]{0:T(256)} %reduce_sum.186, f32[192]{0:T(256)} %reduce_sum.188, f32[147456]{0:T(1024)} %reshape.245, f32[768]{0:T(1024)} %convert_reduce_fusion.2, f32[589824]{0:T(1024)S(1)} %copy-done.9, f32[768]{0:T(1024)} %get-tuple-element.321, f32[589824]{0:T(1024)} %reshape.247, ...), dimensions={0} | concatenate | bytes 14177280 | tf_op jit(solution)/shard_map/concatenate | solution.py:248
  1333.6 95.4 %all-reduce.3.cloned.1.call-done = f32[1772160]{0:T(1024)} async-done(((f32[1772160]{0:T(1024)}), f32[1772160]{0:T(1024)}) %all-reduce.3.cloned.1.call-update) | async-done | bytes 7088656 | tf_op jit(solution)/shard_map/psum | solution.py:249
  1431.1 162.1 %reduce-scatter.11.cloned.1.call-done = f32[768,768]{1,0:T(8,128)} async-done(((f32[3072,768]{1,0:T(8,128)}), f32[768,768]{1,0:T(8,128)}) %reduce-scatter.11.cloned.1.call-update) | async-done | bytes 2359312 | tf_op jit(solution)/shard_map/reduce_scatter | solution.py:216
  1624.0 52.8 %all-reduce = (f32[768]{0:T(1024)}, f32[768]{0:T(1024)}, f32[768]{0:T(1024)}, f32[768]{0:T(1024)}) all-reduce(f32[768]{0:T(1024)S(1)} %get-tuple-element.246, f32[768]{0:T(1024)S(1)} %get-tuple-element.253, f32[768]{0:T(1024)S(1)} %copy-done.28, f32[768]{0:T(1024)S(1)} %copy-done.29), channel_id=1, replica_groups=mesh['dp'=8,'mp'=4] {'dp','mp'}, use_global_device_ids=true, to_apply=%region_20.21 | all-reduce | flops 3072 | bytes 24576 | tf_op jit(solution)/shard_map/psum | solution.py:234
  1676.8 92.3 %all-gather.11.cloned.1.call-done = f32[3072,768]{1,0:T(8,128)} async-done(((f32[768,768]{1,0:T(8,128)}), f32[3072,768]{1,0:T(8,128)}) %all-gather.11.cloned.1.call-update) | async-done | bytes 9437200 | tf_op jit(solution)/shard_map/all_gather | solution.py:231
  (267 shorter events, 481.3 us)
Async XLA Ops:
  7.2 487.9 %copy-start = (bf16[768,768]{1,0:T(8,128)(2,1)S(1)}, bf16[768,768]{1,0:T(8,128)(2,1)}, u32[]{:S(2)}) copy-start(bf16[768,768]{1,0:T(8,128)(2,1)} %param.31) | copy-start | bytes 3538948
  7.2 392.8 %reduce-scatter.5.cloned.1.call-start = ((), (), s32[]{:S(2)}) async-start(), calls=%async_computation.4 | async-start | bytes 11796480 | tf_op jit(solution)/shard_map/reduce_scatter | solution.py:142
  46.0 11.3 copy-start.16
  79.7 11.3 copy-start.16
  113.3 11.3 copy-start.16
  147.0 11.3 copy-start.16
  180.7 11.3 copy-start.16
  214.4 11.3 copy-start.16
  226.3 9.6 copy-start.3
  226.3 9.6 copy-start.6
  235.9 259.2 %all-gather.5.cloned.1.call-start = ((), (), s32[]{:S(2)}) async-start(), calls=%async_computation.5 | async-start | bytes 5898240 | tf_op jit(solution)/shard_map/all_gather | solution.py:152
  236.3 163.6 %copy-start.30 = (f32[768]{0:T(1024)S(1)}, f32[768]{0:T(1024)}, u32[]{:S(2)}) copy-start(f32[768]{0:T(1024)} %param.28) | copy-start | bytes 9220
  243.1 160.0 %copy-start.25 = (f32[768]{0:T(1024)S(1)}, f32[768]{0:T(1024)}, u32[]{:S(2)}) copy-start(f32[768]{0:T(1024)} %param.29) | copy-start | bytes 9220
  243.1 160.0 %copy-start.31 = (f32[768]{0:T(1024)S(1)}, f32[768]{0:T(1024)}, u32[]{:S(2)}) copy-start(f32[768]{0:T(1024)} %param.30) | copy-start | bytes 9220
  404.6 298.0 %reduce-scatter.9.cloned.1.call-start = ((), (), s32[]{:S(2)}) async-start(), calls=%async_computation.8 | async-start | bytes 11796480 | tf_op jit(solution)/shard_map/reduce_scatter | solution.py:180
  405.9 115.7 %copy-start.38 = (f32[768]{0:T(1024)S(1)}, f32[768]{0:T(1024)}, u32[]{:S(2)}) copy-start(f32[768]{0:T(1024)} %param.32) | copy-start | bytes 9220
  495.1 26.5 %copy-start.23 = (f32[3072]{0:T(1024)S(1)}, f32[3072]{0:T(1024)}, u32[]{:S(2)}) copy-start(f32[3072]{0:T(1024)} %fusion.51) | copy-start | bytes 36868
  495.1 26.5 %copy-start.35 = (bf16[768,768]{1,0:T(8,128)(2,1)S(1)}, bf16[768,768]{1,0:T(8,128)(2,1)}, u32[]{:S(2)}) copy-start(bf16[768,768]{1,0:T(8,128)(2,1)} %param.33) | copy-start | bytes 3538948
  542.8 248.2 %reduce-scatter.7.cloned.1.call-start = ((), (), s32[]{:S(2)}) async-start(), calls=%async_computation.6 | async-start | bytes 5898240 | tf_op jit(solution)/shard_map/reduce_scatter | solution.py:159
  551.9 333.8 %all-gather.9.cloned.1.call-start = ((), (), s32[]{:S(2)}) async-start(), calls=%async_computation.9 | async-start | bytes 5898240 | tf_op jit(solution)/shard_map/all_gather | solution.py:190
  560.2 230.8 %copy-start.32 = (f32[768]{0:T(1024)S(1)}, f32[768]{0:T(1024)}, u32[]{:S(2)}) copy-start(f32[768]{0:T(1024)} %param.34) | copy-start | bytes 9220
  795.7 538.0 %all-gather.7.cloned.1.call-start = ((), (), s32[]{:S(2)}) async-start(), calls=%async_computation.7 | async-start | bytes 5898240 | tf_op jit(solution)/shard_map/all_gather | solution.py:167
  820.6 70.2 %copy-start.4 = (bf16[3072,3,64]{0,2,1:T(8,128)(2,1)S(1)}, bf16[3072,3,64]{0,2,1:T(8,128)(2,1)}, u32[]{:S(2)}) copy-start(bf16[3072,3,64]{0,2,1:T(8,128)(2,1)} %copy-done.3) | copy-start | bytes 3538948
  820.6 608.5 %all-reduce.3.cloned.1.call-start = ((), (), s32[]{:S(2)}) async-start(), calls=%async_computation.12 | async-start | bytes 14180352 | tf_op jit(solution)/shard_map/psum | solution.py:249
  1236.0 9.0 copy-start.12
  1249.2 8.5 copy-start.9
  1317.2 276.0 %reduce-scatter.11.cloned.1.call-start = ((), (), s32[]{:S(2)}) async-start(), calls=%async_computation.10 | async-start | bytes 11796480 | tf_op jit(solution)/shard_map/reduce_scatter | solution.py:216
  1326.4 442.7 %all-gather.11.cloned.1.call-start = ((), (), s32[]{:S(2)}) async-start(), calls=%async_computation.11 | async-start | bytes 11796480 | tf_op jit(solution)/shard_map/all_gather | solution.py:231
  1333.6 262.9 %copy-start.11 = (f32[768,768]{1,0:T(8,128)S(1)}, f32[768,768]{1,0:T(8,128)}, u32[]{:S(2)}) copy-start(f32[768,768]{1,0:T(8,128)} %get-tuple-element.299) | copy-start | bytes 7077892
  1615.4 8.6 copy-start.28
  1615.4 8.6 copy-start.29
  1769.1 6.8 copy-start.8
  (29 other events, 115.6 us)
Sparse Core Ops, SparseCore 0:
  236.0 163.9 reduce-scatter.4
  404.7 90.3 all-gather.4
  542.9 159.5 reduce-scatter.8
  704.7 86.2 reduce-scatter.6
  795.8 89.8 all-gather.8
  887.1 87.7 all-gather.6
  1317.4 111.6 all-reduce.2
  1432.0 161.1 reduce-scatter.10
  1600.3 168.7 all-gather.10
where the time goes:
time: 1800 us; the launch traced here: 1790 us
  waiting for transfers between devices  889 us (49%)
  matrix products  409 us (23%)
  other arithmetic  217 us (12%)
  local copies, waits for them, and re-layouts  182 us (10%)
  blocking collectives  52.8 us (3%)
  loops' own time  20.7 us (1%)
    reduce_scatter x1, waiting for transfers between devices, per_device(): lax.psum_scatter(jnp.einsum('ocg,yog->cy', segment_ids, query_key_value_w...  162 us
    reduce_scatter x1, waiting for transfers between devices, per_device(): lax.psum_scatter(jnp.dot(segment_ids, w_out, preferred_element_type=jnp.f...  157 us
    reduce_scatter x1, waiting for transfers between devices, per_device(): lax.psum_scatter(jnp.einsum('tf,df->td', segment_ids, w_up, preferred_ele...  142 us
    psum x1, waiting for transfers between devices, per_device(): summed = lax.psum(flattened_grads, 'dp')  95.4 us
    all_gather x1, waiting for transfers between devices, per_device(): lax.all_gather(grad_input, 'mp', axis=0, tiled=True)  92.3 us
    all_gather x1, waiting for transfers between devices, per_device(): segment_ids = lax.all_gather(second_share, 'mp', axis=0, tiled=True)  89.2 us
    reduce_scatter x1, waiting for transfers between devices, per_device(): lax.psum_scatter(jnp.dot(segment_ids, w_down, preferred_element_type=jnp....  85.2 us
    convert_element_type x6, other arithmetic, compute(): grad_scores = (weights * (grad_weights - row_dot)).astype(jnp.bfloat16)  81.6 us
  transfers between devices with their start and end apart: 9, of which 8 were waited for; matrix products, arithmetic and copies ran while one was open for 26% of the time, Pallas kernels for 0%

commit v1 on v0

v1 whole, which is shorter than its diff:
```python
import functools

import jax
import jax.numpy as jnp
from jax import lax
from jax.experimental import pallas as pl
from jax.experimental.pallas import tpu as pltpu
from jax.sharding import PartitionSpec as P

HEAD_DIM = 64
LOG2E = 1.4426950408889634
EPS = 1e-05
BF = jnp.bfloat16
F32 = jnp.float32
NN = (((1,), (0,)), ((), ()))
NT = (((1,), (1,)), ((), ()))
TN = (((0,), (0,)), ((), ()))
VMEM_LIMIT = 62 * 2**20
MESH = pl.DeviceIdType.MESH


def mm(a, b, dims):
    return lax.dot_general(a, b, dims, preferred_element_type=F32)


def split3(v):
    a = v.astype(BF)
    rest = v - a.astype(F32)
    b = rest.astype(BF)
    return (a, b, (rest - b.astype(F32)).astype(BF))


def normed(rows):
    centred = rows - jnp.mean(rows, axis=-1, keepdims=True)
    inverse = lax.rsqrt(jnp.mean(centred * centred, axis=-1, keepdims=True) + EPS)
    return (centred * inverse, inverse)


def norm_back(grad, n, inverse, gain):
    t = grad * gain
    return inverse * (
        t - jnp.mean(t, axis=-1, keepdims=True) - n * jnp.mean(t * n, axis=-1, keepdims=True)
    )


def row_terms(v, count, width):
    a, b, c = split3(v)
    index = lax.broadcasted_iota(jnp.int32, (count, width), 0)
    spread = lambda t: jnp.broadcast_to(t.astype(F32), (count, width))
    zero = jnp.zeros((count, width), F32)
    picked = jnp.where(index == 2, spread(c), zero)
    picked = jnp.where(index == 1, spread(b), picked)
    return jnp.where(index == 0, spread(a), picked).astype(BF)


def front_kernel(in_ref, w_ref, bias_ref, gain_ref, first_ref, q_ref, k_ref, v_ref, *, width):
    n, _ = normed(in_ref[...].astype(F32))
    first = (n * gain_ref[0:1] + gain_ref[1:2]).astype(BF)
    first_ref[...] = first
    projected = mm(w_ref[...], first, NT) + bias_ref[...]
    q_ref[...] = projected[:width].astype(BF)
    k_ref[...] = projected[width : 2 * width].astype(BF)
    v_ref[...] = projected[2 * width :].astype(BF)


def front(rows, weight, bias, gains, block=512):
    count, features = rows.shape
    width = weight.shape[0] // 3
    row_spec = pl.BlockSpec((block, features), lambda i: (i, 0))
    out_spec = pl.BlockSpec((width, block), lambda i: (0, i))
    return pl.pallas_call(
        functools.partial(front_kernel, width=width),
        grid=(count // block,),
        in_specs=[
            row_spec,
            pl.BlockSpec(weight.shape, lambda i: (0, 0)),
            pl.BlockSpec(bias.shape, lambda i: (0, 0)),
            pl.BlockSpec(gains.shape, lambda i: (0, 0)),
        ],
        out_specs=[row_spec, out_spec, out_spec, out_spec],
        out_shape=[jax.ShapeDtypeStruct((count, features), BF)]
        + [jax.ShapeDtypeStruct((width, count), BF)] * 3,
        compiler_params=pltpu.CompilerParams(vmem_limit_bytes=VMEM_LIMIT),
        name="front",
    )(rows, weight, bias, gains)


def scaled_query(q):
    scaled = q.astype(F32) * (LOG2E * HEAD_DIM**-0.5)
    high = scaled.astype(BF)
    return (high, (scaled - high.astype(F32)).astype(BF))


def extended_keys(k, mask, with_ones):
    count = k.shape[1]
    index = lax.broadcasted_iota(jnp.int32, (128, count), 0)
    rest = 1.0 if with_ones else 0.0
    extra = jnp.where(
        index == 0,
        jnp.broadcast_to(mask, (128, count)),
        jnp.where((index >= 16) & (index < 19), rest, 0.0),
    )
    return (jnp.concatenate([k, k], axis=0).T, extra.astype(BF).T)


def attend_kernel(mask_ref, q_ref, k_ref, v_ref, ctx_ref, total_ref, keys, values, *, block):
    count = k_ref.shape[1]
    width = q_ref.shape[1]

    @pl.when(pl.program_id(1) == 0)
    def _():
        low, high = extended_keys(k_ref[...], mask_ref[...], False)
        keys[:, :128] = low
        keys[:, 128:] = high
        values[:HEAD_DIM] = v_ref[...]
        values[HEAD_DIM:] = jnp.ones((16, count), BF)

    high, low = scaled_query(q_ref[...])
    query = jnp.concatenate([high, low, jnp.ones((128, width), BF)], axis=0)
    top = jnp.full((1, width), -1e30, F32)
    acc = jnp.zeros((HEAD_DIM + 16, width), F32)
    for j in range(count // block):
        part = pl.ds(j * block, block)
        scores = mm(keys[part, :], query, NN)
        new_top = jnp.maximum(top, jnp.max(scores, axis=0, keepdims=True))
        powers = jnp.exp2(scores - new_top).astype(BF)
        acc = acc * jnp.exp2(top - new_top) + mm(values[:, part], powers, NN)
        top = new_top
    total = acc[HEAD_DIM : HEAD_DIM + 1]
    ctx_ref[...] = (acc[:HEAD_DIM] / total).astype(BF)
    total_ref[...] = (top + jnp.log2(total))[None]


def attend(mask, q, k, v, query_block=3072, block=256):
    width, count = q.shape
    heads = width // HEAD_DIM
    query_block = min(query_block, count)
    q_spec = pl.BlockSpec((HEAD_DIM, query_block), lambda h, i: (h, i))
    k_spec = pl.BlockSpec((HEAD_DIM, count), lambda h, i: (h, 0))
    return pl.pallas_call(
        functools.partial(attend_kernel, block=block),
        grid=(heads, count // query_block),
        in_specs=[pl.BlockSpec((1, count), lambda h, i: (0, 0)), q_spec, k_spec, k_spec],
        out_specs=[q_spec, pl.BlockSpec((1, 1, query_block), lambda h, i: (h, 0, i))],
        out_shape=[
            jax.ShapeDtypeStruct((width, count), BF),
            jax.ShapeDtypeStruct((heads, 1, count), F32),
        ],
        scratch_shapes=[pltpu.VMEM((count, 256), BF), pltpu.VMEM((HEAD_DIM + 16, count), BF)],
        compiler_params=pltpu.CompilerParams(vmem_limit_bytes=VMEM_LIMIT),
        name="attend",
    )(mask, q, k, v)


def attend_back_kernel(
    mask_ref, q_ref, k_ref, v_ref, ctx_ref, g_ref, total_ref,
    dq_ref, dk_ref, dv_ref, keys, values, dk_acc, dv_acc, *, block,
):
    count = k_ref.shape[1]
    width = q_ref.shape[1]

    @pl.when(pl.program_id(1) == 0)
    def _():
        low, high = extended_keys(k_ref[...], mask_ref[...], True)
        keys[:, :128] = low
        keys[:, 128:] = high
        values[...] = jnp.concatenate([v_ref[...], jnp.ones((HEAD_DIM, count), BF)], axis=0).T
        dk_acc[...] = jnp.zeros_like(dk_acc)
        dv_acc[...] = jnp.zeros_like(dv_acc)

    q = q_ref[...]
    g = g_ref[...]
    high, low = scaled_query(q)
    dots = jnp.sum(g.astype(F32) * ctx_ref[...].astype(F32), axis=0, keepdims=True)
    query = jnp.concatenate(
        [high, low, jnp.ones((16, width), BF), row_terms(-total_ref[0], 112, width)], axis=0
    )
    grads = jnp.concatenate([g, row_terms(-dots, HEAD_DIM, width)], axis=0)
    dq = jnp.zeros((HEAD_DIM, width), F32)
    for j in range(count // block):
        part = pl.ds(j * block, block)
        probs = jnp.exp2(mm(keys[part, :], query, NN))
        probs_low = probs.astype(BF)
        grad_scores = (probs * mm(values[part, :], grads, NN)).astype(BF)
        dv_acc[:, part] += mm(g, probs_low, NT)
        dk_acc[:, part] += mm(q, grad_scores, NT)
        dq = dq + mm(k_ref[:, part], grad_scores, NN)
    dq_ref[...] = (dq * HEAD_DIM**-0.5).astype(BF)

    @pl.when(pl.program_id(1) == pl.num_programs(1) - 1)
    def _():
        dk_ref[...] = (dk_acc[...] * HEAD_DIM**-0.5).astype(BF)
        dv_ref[...] = dv_acc[...].astype(BF)


def attend_back(mask, q, k, v, ctx, g, totals, query_block=1024, block=256):
    width, count = q.shape
    heads = width // HEAD_DIM
    q_spec = pl.BlockSpec((HEAD_DIM, query_block), lambda h, i: (h, i))
    k_spec = pl.BlockSpec((HEAD_DIM, count), lambda h, i: (h, 0))
    return pl.pallas_call(
        functools.partial(attend_back_kernel, block=block),
        grid=(heads, count // query_block),
        in_specs=[
            pl.BlockSpec((1, count), lambda h, i: (0, 0)), q_spec, k_spec, k_spec, q_spec, q_spec,
            pl.BlockSpec((1, 1, query_block), lambda h, i: (h, 0, i)),
        ],
        out_specs=[q_spec, k_spec, k_spec],
        out_shape=[jax.ShapeDtypeStruct((width, count), BF)] * 3,
        scratch_shapes=[
            pltpu.VMEM((count, 256), BF),
            pltpu.VMEM((count, 2 * HEAD_DIM), BF),
            pltpu.VMEM((HEAD_DIM, count), F32),
            pltpu.VMEM((HEAD_DIM, count), F32),
        ],
        compiler_params=pltpu.CompilerParams(vmem_limit_bytes=VMEM_LIMIT),
        name="attend_back",
    )(mask, q, k, v, ctx, g, totals)


def middle_kernel(
    count_ref, ctx_ref, in_ref, grad_ref, w_ref, vec_ref,
    out_ref, mixed_grad_ref, ctx_grad_ref, low_sums_ref, rows_ref, sums_ref, outer_ref,
    *, parts, hidden, width,
):
    me = lax.axis_index("mp")
    step = pl.program_id(0)
    block, features = in_ref.shape
    down, outer, tail = features, features + hidden, features + hidden + width
    pieces = w_ref.shape[1]

    def shard(s, start, size):
        low = start // pieces
        return w_ref[s, :, low : low + size // pieces, :].reshape(size, features)


    @pl.when(step == 0)
    def _():
        sums_ref[...] = jnp.zeros_like(sums_ref)
        rows_ref[...] = jnp.zeros_like(rows_ref)
        for s in range(parts):
            outer_ref[s * width : (s + 1) * width, :] = shard(s, outer, width)

    mixed = in_ref[...].astype(F32) + vec_ref[0:1] + mm(ctx_ref[...], outer_ref[...], TN)
    n, inverse = normed(mixed)
    second = (n * vec_ref[1:2] + vec_ref[2:3]).astype(BF)
    row = step * block + lax.broadcasted_iota(jnp.int32, (block, 1), 0)
    grad_y = jnp.where(row < count_ref[0], grad_ref[...].astype(F32), 0.0)
    grad_low = grad_y.astype(BF)
    out = mixed + vec_ref[3:4]
    grad_second = jnp.zeros((block, features), F32)
    for turn in range(parts):
        s = lax.rem(me + turn, parts)
        w_up = shard(s, 0, features)
        w_down = shard(s, down, hidden)
        terms = w_ref[s, 0, tail // pieces : tail // pieces + 8, :].astype(F32)
        up = mm(second, w_up, NN) + (terms[0:1] + terms[1:2] + terms[2:3])
        grad_act = mm(grad_low, w_down, NT)
        below = 0.5 * lax.erf(up * 0.7071067811865476) + 0.5
        density = jnp.exp2(up * up * (-0.5 * LOG2E)) * 0.3989422804014327
        activated = (up * below).astype(BF)
        grad_up = (grad_act * (below + up * density)).astype(BF)
        out = out + mm(activated, w_down, NN)
        grad_second = grad_second + mm(grad_up, w_up, NT)
        if turn == 0:
            sums_ref[0:features, :] += mm(second, grad_up, TN)
            sums_ref[down : down + hidden, :] += mm(activated, grad_low, TN)
            rows_ref[4:5, :] += jnp.sum(
                grad_up.astype(F32), axis=0, keepdims=True
            )
    out_ref[...] = out.astype(BF)
    grad_mixed = grad_y + norm_back(grad_second, n, inverse, vec_ref[1:2])
    mixed_grad_ref[...] = grad_mixed
    mixed_low = grad_mixed.astype(BF)
    own = pl.ds(me * width, width)
    ctx_grad_ref[...] = mm(outer_ref[own, :], mixed_low, NT).astype(BF)
    sums_ref[outer : outer + width, :] += mm(
        ctx_ref[own, :], mixed_low, NN
    )
    rows_ref[0:4, :] += jnp.concatenate(
        [
            jnp.sum(mixed_low.astype(F32), axis=0, keepdims=True),
            jnp.sum(grad_low.astype(F32), axis=0, keepdims=True),
            jnp.sum(grad_second * n, axis=0, keepdims=True),
            jnp.sum(grad_second, axis=0, keepdims=True),
        ],
        axis=0,
    )

    @pl.when(step == pl.num_programs(0) - 1)
    def _():
        low_sums_ref[:tail] = sums_ref[...].astype(BF)
        low_sums_ref[tail:] = jnp.zeros((low_sums_ref.shape[0] - tail, features), BF)


def middle(counts, ctx, rows, grads, weights, vectors, hidden, width, held, block=512):
    count, features = rows.shape
    parts = weights.shape[0]
    row_spec = pl.BlockSpec((block, features), lambda i: (i, 0))
    sums = features + hidden + width
    return pl.pallas_call(
        functools.partial(middle_kernel, parts=parts, hidden=hidden, width=width),
        grid=(count // block,),
        in_specs=[
            pl.BlockSpec(memory_space=pltpu.SMEM),
            pl.BlockSpec((parts * width, block), lambda i: (0, i)),
            row_spec,
            row_spec,
            pl.BlockSpec(weights.shape, lambda i: (0, 0, 0, 0), pipeline_mode=pl.Buffered(1)),
            pl.BlockSpec(vectors.shape, lambda i: (0, 0)),
        ],
        out_specs=[
            row_spec,
            row_spec,
            pl.BlockSpec((width, block), lambda i: (0, i)),
            pl.BlockSpec((held, features), lambda i: (0, 0), pipeline_mode=pl.Buffered(1)),
            pl.BlockSpec((8, features), lambda i: (0, 0)),
        ],
        out_shape=[
            jax.ShapeDtypeStruct((count, features), BF),
            jax.ShapeDtypeStruct((count, features), F32),
            jax.ShapeDtypeStruct((width, count), BF),
            jax.ShapeDtypeStruct((held, features), BF),
            jax.ShapeDtypeStruct((8, features), F32),
        ],
        scratch_shapes=[
            pltpu.VMEM((sums, features), F32), pltpu.VMEM((parts * width, features), BF)
        ],
        compiler_params=pltpu.CompilerParams(vmem_limit_bytes=VMEM_LIMIT),
        name="middle",
    )(counts, ctx, rows, grads, weights, vectors)


def project_back_kernel(
    first_ref, rows_ref, dq_ref, dk_ref, dv_ref, w_ref, small_ref, held_ref,
    part_ref, vec_ref, all_ref, sums_ref, low_ref, sem, *, width, start,
):
    step = pl.program_id(0)

    @pl.when(step == 0)
    def _():
        sums_ref[...] = jnp.zeros_like(sums_ref)
        vec_ref[0:8] = jnp.zeros_like(small_ref)
        vec_ref[8:16] = small_ref[...]
        vec_ref[16:24] = jnp.zeros_like(small_ref)

    grads = jnp.concatenate([dq_ref[...], dk_ref[...], dv_ref[...]], axis=0)
    partial = mm(grads, w_ref[...], TN)
    part_ref[...] = partial.astype(BF)
    n, _ = normed(rows_ref[...].astype(F32))
    vec_ref[0:1] += jnp.sum(partial * n, axis=0, keepdims=True)
    vec_ref[1:2] += jnp.sum(partial, axis=0, keepdims=True)
    sums_ref[...] += mm(grads, first_ref[...], NN)
    ones = jnp.ones((8, grads.shape[1]), BF)
    vec_ref[16:24, : 3 * width] += mm(ones, grads, NT)

    @pl.when(step == pl.num_programs(0) - 1)
    def _():
        low_ref[...] = sums_ref[...].astype(BF)
        copy = pltpu.make_async_copy(low_ref, all_ref.at[pl.ds(start, 3 * width)], sem)
        copy.start()
        copy.wait()


def project_back(first, rows, dq, dk, dv, weight, small, held, start, block=512):
    count, features = first.shape
    width = dq.shape[0]
    row_spec = pl.BlockSpec((block, features), lambda i: (i, 0))
    d_spec = pl.BlockSpec((width, block), lambda i: (0, i))
    whole = lambda t: pl.BlockSpec(t.shape, lambda i: (0, 0))
    return pl.pallas_call(
        functools.partial(project_back_kernel, width=width, start=start),
        grid=(count // block,),
        in_specs=[
            row_spec, row_spec, d_spec, d_spec, d_spec, whole(weight), whole(small),
            pl.BlockSpec(memory_space=pl.ANY),
        ],
        out_specs=[
            row_spec,
            pl.BlockSpec((24, features), lambda i: (0, 0)),
            pl.BlockSpec(memory_space=pl.ANY),
        ],
        out_shape=[
            jax.ShapeDtypeStruct((count, features), BF),
            jax.ShapeDtypeStruct((24, features), F32),
            jax.ShapeDtypeStruct(held.shape, BF),
        ],
        scratch_shapes=[
            pltpu.VMEM((3 * width, features), F32),
            pltpu.VMEM((3 * width, features), BF),
            pltpu.SemaphoreType.DMA,
        ],
        input_output_aliases={7: 2},
        compiler_params=pltpu.CompilerParams(vmem_limit_bytes=VMEM_LIMIT),
        name="project_back",
    )(first, rows, dq, dk, dv, weight, small, held)


def finish_kernel(
    part_ref, all_rows_ref, all_mixed_ref, gain_ref, norm_ref, sums_ref,
    out_ref, total_ref, sum_out,
    rows_ref, mixed_ref, own_sems, from_left, from_right, sum_left, sum_right, sum_send_right, sum_send_left,
    row_left, row_right, row_send_right, row_send_left,
    group_norm, all_norm, sum_in, group_send, group_recv, all_send, all_recv,
    piece_send, piece_recv, done_send, done_recv, *, parts, copies,
):
    me = lax.axis_index("mp")
    chunks = part_ref.shape[1]
    first, last = me == 0, me == parts - 1

    def send(source, target, send_sem, recv_sem, step):
        return pltpu.make_async_remote_copy(
            src_ref=source, dst_ref=target, send_sem=send_sem, recv_sem=recv_sem,
            device_id={"mp": lax.rem(me + step + parts, parts)},
            device_id_type=MESH,
        )

    def sum_copy(k, c, step, source):
        if step > 0:
            return send(source, from_left.at[k - 1, c], sum_send_right.at[k - 1, c], sum_left.at[k - 1, c], 1)
        return send(source, from_right.at[k - 1, c], sum_send_left.at[k - 1, c], sum_right.at[k - 1, c], -1)

    def row_copy(j, c, step):
        owner = lax.rem(me - step * j + parts, parts)
        block = out_ref.at[owner, c]
        if step > 0:
            return send(block, block, row_send_right.at[j, c], row_left.at[j, c], 1)
        return send(block, block, row_send_left.at[j, c], row_right.at[j, c], -1)

    own_copies = (
        pltpu.make_async_copy(all_rows_ref.at[me], rows_ref, own_sems.at[0]),
        pltpu.make_async_copy(all_mixed_ref.at[me], mixed_ref, own_sems.at[1]),
    )
    for copy in own_copies:
        copy.start()
    cell = lax.axis_index("dp")
    small = group_norm.shape[1]

    def to_group(j, source, target, send_sem, recv_sem):
        return pltpu.make_async_remote_copy(
            src_ref=source, dst_ref=target, send_sem=send_sem, recv_sem=recv_sem,
            device_id={"mp": lax.rem(me + j, parts)}, device_id_type=MESH,
        )

    def to_cell(j, source, target, send_sem, recv_sem):
        return pltpu.make_async_remote_copy(
            src_ref=source, dst_ref=target, send_sem=send_sem, recv_sem=recv_sem,
            device_id={"dp": lax.rem(cell + j, copies)}, device_id_type=MESH,
        )

    def group_copy(j, source):
        return to_group(
            j, norm_ref.at[pl.ds(0, small)], group_norm.at[source], group_send.at[j], group_recv.at[source]
        )

    def cell_copy(j, source):
        return to_cell(j, total_ref, all_norm.at[source], all_send.at[j], all_recv.at[source])

    def piece_copy(j, source):
        return to_cell(
            j, sums_ref.at[lax.rem(cell + j, copies)], sum_in.at[source],
            piece_send.at[j], piece_recv.at[source],
        )

    def done_copy(j, source):
        return to_cell(
            j, sum_out.at[source], sum_out.at[source], done_send.at[j], done_recv.at[source]
        )

    def each(then, end):
        lax.fori_loop(1, end, lambda j, carry: (then(j), carry)[1], 0)

    behind = lambda j: lax.rem(cell - j + copies, copies)

    def summed(ref, end):
        return lax.fori_loop(1, end, lambda j, total: total + ref[j], ref[0])

    barrier = pltpu.get_barrier_semaphore()
    each(lambda j: pl.semaphore_signal(
        barrier, inc=1, device_id={"mp": lax.rem(me + j, parts)}, device_id_type=MESH), parts)
    each(lambda j: pl.semaphore_signal(
        barrier, inc=1, device_id={"dp": lax.rem(cell + j, copies)}, device_id_type=MESH), copies)
    pl.semaphore_wait(barrier, parts + copies - 2)
    each(lambda j: group_copy(j, me).start(), parts)
    each(lambda j: piece_copy(j, cell).start(), copies)
    group_norm[me] = norm_ref[0:small]

    def group_total():
        each(lambda j: group_copy(j, lax.rem(me - j + parts, parts)).wait(), parts)
        total_ref[0:small] = summed(group_norm, parts)
        total_ref[small:] = norm_ref[small:]
        all_norm[cell] = total_ref[...]
        each(lambda j: cell_copy(j, cell).start(), copies)

    def piece_total():
        each(lambda j: piece_copy(j, behind(j)).wait(), copies)
        total = lax.fori_loop(
            1, copies, lambda j, total: total + sum_in[behind(j)].astype(F32), sums_ref[cell].astype(F32)
        )
        sum_out[cell] = total.astype(BF)
        each(lambda j: done_copy(j, cell).start(), copies)

    for copy in own_copies:
        copy.wait()

    def pass_sums(step, c):
        place = me if step > 0 else parts - 1 - me
        slots = from_left if step > 0 else from_right
        for k in range(parts - 1, 0, -1):
            owner = lax.rem(me + step * k + parts, parts)

            @pl.when(place == 0)
            def _():
                sum_copy(k, c, step, part_ref.at[owner, c]).start()

            if k < parts - 1:

                @pl.when((place > 0) & (place + k < parts))
                def _():
                    sum_copy(k + 1, c, step, part_ref.at[owner, c]).wait_recv()
                    slots[k, c] = (
                        slots[k, c].astype(F32) + part_ref[owner, c].astype(F32)
                    ).astype(BF)
                    sum_copy(k, c, step, slots.at[k, c]).start()

    def finish(c):
        @pl.when(jnp.logical_not(first))
        def _():
            sum_copy(1, c, 1, part_ref.at[0, c]).wait_recv()

        @pl.when(jnp.logical_not(last))
        def _():
            sum_copy(1, c, -1, part_ref.at[0, c]).wait_recv()

        grad = part_ref[me, c].astype(F32)
        zero = jnp.zeros_like(grad)
        grad = grad + jnp.where(first, zero, from_left[0, c].astype(F32))
        grad = grad + jnp.where(last, zero, from_right[0, c].astype(F32))
        n, inverse = normed(rows_ref[c].astype(F32))
        out_ref[me, c] = (mixed_ref[c] + norm_back(grad, n, inverse, gain_ref[...])).astype(BF)

        @pl.when(jnp.logical_not(last))
        def _():
            row_copy(0, c, 1).start()

        @pl.when(jnp.logical_not(first))
        def _():
            row_copy(0, c, -1).start()

    def pass_rows(step, j, c):
        place = me if step > 0 else parts - 1 - me

        @pl.when(place >= j + 1)
        def _():
            owner = lax.rem(me - step * (j + 1) + 2 * parts, parts)
            block = out_ref.at[owner, c]
            if step > 0:
                arrival = send(block, block, row_send_right.at[j, c], row_left.at[j, c], 1)
            else:
                arrival = send(block, block, row_send_left.at[j, c], row_right.at[j, c], -1)
            arrival.wait_recv()

        if j + 1 < parts - 1:

            @pl.when((place >= j + 1) & (place < parts - 1))
            def _():
                row_copy(j + 1, c, step).start()

    def within(c, then):
        @pl.when((c >= 0) & (c < chunks))
        def _():
            then(c)

    def turn(t, carry):
        within(t - me, lambda c: pass_sums(1, c))
        within(t - (parts - 1 - me), lambda c: pass_sums(-1, c))
        within(t - (parts - 1), finish)
        for j in range(parts - 1):
            within(t - (parts + j), lambda c: pass_rows(1, j, c))
            within(t - (parts + j), lambda c: pass_rows(-1, j, c))

        @pl.when(t == parts)
        def _():
            group_total()

        @pl.when(t == parts + chunks // 2)
        def _():
            piece_total()

        return carry

    lax.fori_loop(0, chunks + 2 * parts - 2, turn, 0)

    def drain(c, carry):
        for step in (1, -1):
            place = me if step > 0 else parts - 1 - me
            for k in range(1, parts):

                @pl.when(place + k < parts)
                def _():
                    sum_copy(k, c, step, part_ref.at[0, c]).wait_send()

            for j in range(parts - 1):

                @pl.when((place >= j) & (place < parts - 1))
                def _():
                    row_copy(j, c, step).wait_send()
        return carry

    lax.fori_loop(0, chunks, drain, 0)
    each(lambda j: cell_copy(j, behind(j)).wait(), copies)
    each(lambda j: done_copy(j, behind(j)).wait(), copies)
    total_ref[...] = summed(all_norm, copies)


def finish(partial, rows, mixed_grad, gain, norm_sums, sums, parts, copies, chunks):
    count, features = partial.shape
    size = count // (parts * chunks)
    whole = (parts, chunks, size, features)
    pieces = (copies, sums.shape[0] // copies, features)
    own = pl.BlockSpec(memory_space=pl.ANY)
    full = pl.BlockSpec(memory_space=pltpu.VMEM)
    dma = pltpu.SemaphoreType.DMA
    return pl.pallas_call(
        functools.partial(finish_kernel, parts=parts, copies=copies),
        in_specs=[full, own, own, full, full, full],
        out_specs=[full, full, full],
        out_shape=[
            jax.ShapeDtypeStruct(whole, BF),
            jax.ShapeDtypeStruct(norm_sums.shape, F32),
            jax.ShapeDtypeStruct(pieces, BF),
        ],
        scratch_shapes=[
            pltpu.VMEM((chunks, size, features), BF),
            pltpu.VMEM((chunks, size, features), F32),
            dma((2,)),
        ]
        + [pltpu.VMEM((parts - 1, chunks, size, features), BF)] * 2
        + [dma((parts - 1, chunks)) for _ in range(8)]
        + [
            pltpu.VMEM((parts, 8, features), F32),
            pltpu.VMEM((copies, *norm_sums.shape), F32),
            pltpu.VMEM(pieces, BF),
        ]
        + [dma((number,)) for number in (parts, parts) + (copies,) * 6],
        compiler_params=pltpu.CompilerParams(
            vmem_limit_bytes=VMEM_LIMIT, collective_id=0, has_side_effects=True
        ),
        name="finish",
    )(
        partial.reshape(whole), rows.reshape(whole), mixed_grad.reshape(whole), gain, norm_sums,
        sums.reshape(pieces),
    )


def per_device(
    inputs, counts, first_gain, first_bias, query_key_value_weight, query_bias, value_bias,
    w_out, out_bias, second_gain, second_bias, w_up, up_bias, w_down, down_bias, out_grad,
):
    _, slots, features = inputs.shape
    width = query_key_value_weight.shape[2]
    hidden = w_up.shape[1]
    parts = lax.axis_size("mp")
    copies = lax.axis_size("dp")
    rows = inputs.reshape(slots, features)
    grads = out_grad.reshape(slots, features)

    bias_terms = jnp.concatenate(
        [jnp.stack(split3(up_bias)), jnp.zeros((5, features), BF)], axis=0
    )
    if width % (8 * copies) == 0 and features % (8 * copies) == 0 and hidden % (8 * copies) == 0:
        pieces = copies
        cut = lambda t: lax.dynamic_slice_in_dim(
            t, lax.axis_index("dp") * (t.shape[0] // copies), t.shape[0] // copies, 0
        )
        piece = jnp.concatenate([cut(w_up), cut(w_down), cut(w_out), bias_terms], axis=0)
    else:
        pieces = 1
        used = features + hidden + width + 8
        padded = -(-used // (16 * copies)) * 16 * copies
        shard = jnp.concatenate(
            [w_up, w_down, w_out, bias_terms, jnp.zeros((padded - used, features), BF)], axis=0
        )
        piece = lax.dynamic_slice_in_dim(
            shard, lax.axis_index("dp") * (padded // copies), padded // copies, 0
        )
    piece, rows = lax.optimization_barrier((piece, rows))
    weights = lax.all_gather(piece, ("mp", "dp"), axis=0, tiled=True)
    weights = weights.reshape(parts, pieces, -1, features)

    weight = query_key_value_weight.transpose(1, 2, 0).reshape(3 * width, features)
    bias = jnp.concatenate([query_bias, jnp.zeros_like(query_bias), value_bias])[:, None]
    first, q, k, v = front(rows, weight, bias, jnp.stack([first_gain, first_bias]))
    mask = jnp.where(jnp.arange(slots)[None, :] < counts[:, None], 0.0, -1e30).astype(F32)
    ctx, totals = attend(mask, q, k, v)
    ctx, weights = lax.optimization_barrier((ctx, weights))
    all_ctx = lax.all_gather(ctx, "mp", axis=0, tiled=True)
    vectors = jnp.stack([out_bias, second_gain, second_bias, down_bias])
    used = features + hidden + 4 * width
    held = -(-used // (16 * copies)) * 16 * copies
    outputs, grad_mixed, ctx_grad, sums, small = middle(
        counts, all_ctx, rows, grads, weights, vectors, hidden, width, held
    )
    dq, dk, dv = attend_back(mask, q, k, v, ctx, ctx_grad, totals)
    late = features + hidden + width
    partial, vec, sums = project_back(first, rows, dq, dk, dv, weight, small, sums, late)
    chunks = next(c for c in (16, 8, 4, 2, 1) if slots % (8 * parts * c) == 0)
    input_grad, vec, sums = finish(
        partial, rows, grad_mixed, first_gain[None], vec, sums, parts, copies, chunks
    )
    sums = sums.reshape(held, features).astype(F32)
    down, outer = features, features + hidden
    return (
        outputs.reshape(inputs.shape),
        input_grad.reshape(inputs.shape).astype(F32),
        vec[0],
        vec[1],
        sums[late : late + 3 * width].reshape(3, width, features).transpose(2, 0, 1),
        vec[16, :width],
        vec[16, 2 * width : 3 * width],
        sums[outer : outer + width],
        vec[8],
        vec[10],
        vec[11],
        sums[:features],
        vec[12],
        sums[down : down + hidden],
        vec[9],
    )


def solution(mesh):
    row = P("dp", None, None)
    return jax.shard_map(
        per_device,
        mesh=mesh,
        in_specs=(
            row, P("dp"), P(), P(), P(None, None, "mp"), P("mp"), P("mp"), P("mp", None), P(),
            P(), P(), P(None, "mp"), P("mp"), P("mp", None), P(), row,
        ),
        out_specs=(
            row, row, P(), P(), P(None, None, "mp"), P("mp"), P("mp"), P("mp", None), P(),
            P(), P(), P(None, "mp"), P("mp"), P("mp", None), P(),
        ),
        check_vma=False,
    )
```

time: 1800 us -> 540 us (0.30)
  waiting for transfers between devices: 889 us -> 131 us
  matrix products: 409 us -> 0 us
  Pallas kernels: 0 us -> 365 us
  other arithmetic: 217 us -> 8.49 us
  local copies, waits for them, and re-layouts: 182 us -> 15.4 us
  blocking collectives: 52.8 us -> 0 us
  loops' own time: 20.7 us -> 0 us
    reduce_scatter x4 -> x0, waiting for transfers between devices: 547 us -> none  [the longest x1 162 us: per_device(): lax.psum_scatter(jnp.einsum('ocg,yog->cy', segment_ids, query_key_value_w...]
    dot_general x52 -> x0, matrix products: 399 us -> none  [the longest x6 79.7 us: compute(): jnp.einsum('qhd,khd->hqk', grad_block, value_rows, preferred_element_type...]
    pallas_call x0 -> x6, Pallas kernels: none -> 365 us  [the longest x1 134 us: finish(): pl.pallas_call(functools.partial(finish_kernel, parts=parts, copies=copie...]
    all_gather x4 -> x2, waiting for transfers between devices: 247 us -> 131 us  [the longest x1 88.8 us: per_device(): all_ctx = lax.all_gather(ctx, 'mp', axis=0, tiled=True)]
    psum x1 -> x0, waiting for transfers between devices: 95.4 us -> none  [per_device(): summed = lax.psum(flattened_grads, 'dp')]
    reduce_sum x16 -> x0, other arithmetic: 94.5 us -> none  [the longest x6 65.8 us: one_block(): totals = jnp.sum(powers, axis=-1, keepdims=True)]
    convert_element_type x12 -> x3, other arithmetic: 99.1 us -> 5.89 us  [the longest x1 4.48 us: per_device(): input_grad.reshape(inputs.shape).astype(F32)]
    concatenate x1, local copies, waits for them, and re-layouts: 59.5 us -> 2.62 us  [per_device(): jnp.concatenate([cut(w_up), cut(w_down), cut(w_out), bias_terms], axis=0)]
  transfers between devices with their start and end apart: 9 -> 2, of which waited for: 8 -> 2; matrix products, arithmetic and copies ran while one was open for 26% -> 1% of each run, Pallas kernels for 0% -> 8%
where the time goes in v1:
time: 540 us; the launch traced here: 536 us
  Pallas kernels  365 us (68%)
  waiting for transfers between devices  131 us (24%)
  local copies, waits for them, and re-layouts  15.4 us (3%)
  between operations  15.3 us (3%)
  other arithmetic  8.49 us (2%)
    pallas_call x1, Pallas kernels, finish(): pl.pallas_call(functools.partial(finish_kernel, parts=parts, copies=copie...  134 us
    pallas_call x1, Pallas kernels, middle(): pl.pallas_call(functools.partial(middle_kernel, parts=parts, hidden=hidde...  103 us
    all_gather x1, waiting for transfers between devices, per_device(): all_ctx = lax.all_gather(ctx, 'mp', axis=0, tiled=True)  88.8 us
    pallas_call x1, Pallas kernels, attend_back(): pl.pallas_call(functools.partial(attend_back_kernel, block=block), grid=(...  70.4 us
    all_gather x1, waiting for transfers between devices, per_device(): weights = lax.all_gather(piece, ('mp', 'dp'), axis=0, tiled=True)  42.2 us
    pallas_call x1, Pallas kernels, attend(): pl.pallas_call(functools.partial(attend_kernel, block=block), grid=(heads...  34.1 us
    pallas_call x1, Pallas kernels, project_back(): pl.pallas_call(functools.partial(project_back_kernel, width=width, start=...  14 us
  transfers between devices with their start and end apart: 2, of which 2 were waited for; matrix products, arithmetic and copies ran while one was open for 1% of the time, Pallas kernels for 8%

profile of v1, /device:TPU:0, one launch (start us, length us, event | category | flops | bytes accessed | tf_op | source)
XLA Modules:
  0.0 535.8 jit_solution(14602379347139403876)
XLA Ops:
  7.2 0.0 copy-start
  7.2 0.0 all-gather.3.cloned.1.call-start
  7.2 0.8 subtract_convert_fusion
  8.1 0.1 copy-done
  8.2 1.0 constant_dynamic-slice_fusion.1
  9.2 2.6 concatenate.6
  11.8 0.0 all-gather.3.cloned.1.call-update
  11.8 0.0 all-gather.5.cloned.1.call-start
  12.5 0.7 stack.36.gain_ref
  13.2 0.7 stack.37
  13.9 0.8 pad_maximum_fusion.2
  14.7 0.9 broadcast_in_dim.25.bias_ref
  15.5 0.6 pad_maximum_fusion.1.gain_ref
  16.1 9.9 %front.1 = (bf16[3072,768]{1,0:T(8,128)(2,1)}, bf16[192,3072]{1,0:T(8,128)(2,1)}, bf16[192,3072]{1,0:T(8,128)(2,1)}, bf16[192,3072]{1,0:T(8,128)(2,1)}) custom-call(bf16[3072,768]{1,0:T(8,128)(2,1)} %bitcast.21, bf16[576,768]{1,0:T(8,128)(2,1)} %bitcast.35, f32[576,1]{1,0:T(8,128)} %broadcast_in_dim.25.bias_ref, f32[2,768]{1,0:T(2,128)} %pad_maximum_fusion.1.gain_ref), custom_call_target="tpu_custom_call" | custom-call | tf_op jit(solution)/shard_map/front/pallas_call | solution.py:71
  26.1 0.6 compare_select_fusion.mask_ref
  26.7 34.1 %attend.1 = (bf16[192,3072]{1,0:T(8,128)(2,1)}, f32[3,1,3072]{2,1,0:T(1,128)}) custom-call(f32[1,3072]{1,0:T(1,128)} %compare_select_fusion.mask_ref, bf16[192,3072]{1,0:T(8,128)(2,1)} %get-tuple-element.40.q_ref, bf16[192,3072]{1,0:T(8,128)(2,1)} %get-tuple-element.41.k_ref, bf16[192,3072]{1,0:T(8,128)(2,1)} %get-tuple-element.42.v_ref), custom_call_target="tpu_custom_call" | custom-call | tf_op jit(solution)/shard_map/attend/pallas_call | solution.py:140
  60.8 42.2 %all-gather.3.cloned.1.call-done = bf16[7168,768]{1,0:T(8,128)(2,1)} async-done(((bf16[224,768]{1,0:T(8,128)(2,1)}), bf16[7168,768]{1,0:T(8,128)(2,1)}) %all-gather.3.cloned.1.call-update) | async-done | bytes 11010064 | tf_op jit(solution)/shard_map/all_gather | solution.py:688
  103.0 0.0 all-gather.5.cloned.1.call-update
  103.1 0.6 pad_maximum_fusion.vec_ref
  103.7 88.8 %all-gather.5.cloned.1.call-done.ctx_ref = bf16[768,3072]{1,0:T(8,128)(2,1)} async-done(((bf16[192,3072]{1,0:T(8,128)(2,1)}), bf16[768,3072]{1,0:T(8,128)(2,1)}) %all-gather.5.cloned.1.call-update) | async-done | bytes 4718608 | tf_op jit(solution)/shard_map/all_gather | solution.py:697
  192.5 102.9 %middle.1 = (bf16[3072,768]{1,0:T(8,128)(2,1)}, f32[3072,768]{1,0:T(8,128)}, bf16[192,3072]{1,0:T(8,128)(2,1)}, bf16[2304,768]{1,0:T(8,128)(2,1)}, f32[8,768]{1,0:T(8,128)}) custom-call(s32[1]{0:T(128)} %copy.34.count_ref, bf16[768,3072]{1,0:T(8,128)(2,1)} %all-gather.5.cloned.1.call-done.ctx_ref, bf16[3072,768]{1,0:T(8,128)(2,1)} %bitcast.22, ...), custom_call_target="tpu_custom_call" | custom-call | tf_op jit(solution)/shard_map/middle/pallas_call | solution.py:301
  295.5 70.4 %attend_back.1 = (bf16[192,3072]{1,0:T(8,128)(2,1)}, bf16[192,3072]{1,0:T(8,128)(2,1)}, bf16[192,3072]{1,0:T(8,128)(2,1)}) custom-call(f32[1,3072]{1,0:T(1,128)} %compare_select_fusion.mask_ref, bf16[192,3072]{1,0:T(8,128)(2,1)} %get-tuple-element.40.q_ref, bf16[192,3072]{1,0:T(8,128)(2,1)} %get-tuple-element.41.k_ref, ...), custom_call_target="tpu_custom_call" | custom-call | tf_op jit(solution)/shard_map/attend_back/pallas_call | solution.py:201
  365.8 14.0 %project_back.1 = (bf16[3072,768]{1,0:T(8,128)(2,1)}, f32[24,768]{1,0:T(8,128)}, bf16[2304,768]{1,0:T(8,128)(2,1)}) custom-call(bf16[3072,768]{1,0:T(8,128)(2,1)} %get-tuple-element.48.first_ref, bf16[3072,768]{1,0:T(8,128)(2,1)} %bitcast.23, bf16[192,3072]{1,0:T(8,128)(2,1)} %get-tuple-element.51.dq_ref, ...), custom_call_target="tpu_custom_call", output_to_operand_aliasing={{2}: (7, {})} | custom-call | tf_op jit(solution)/shard_map/project_back/pallas_call | solution.py:371
  379.8 134.2 %finish.1 = (bf16[4,16,48,768]{3,2,1,0:T(8,128)(2,1)}, f32[24,768]{1,0:T(8,128)}, bf16[8,288,768]{2,1,0:T(8,128)(2,1)}) custom-call(bf16[4,16,48,768]{3,2,1,0:T(8,128)(2,1)} %bitcast.34, bf16[4,16,48,768]{3,2,1,0:T(8,128)(2,1)} %bitcast.24, f32[4,16,48,768]{3,2,1,0:T(8,128)} %bitcast.29, f32[1,768]{1,0:T(1,128)} %copy-done.3, ...), custom_call_target="tpu_custom_call" | custom-call | tf_op jit(solution)/shard_map/finish/pallas_call | solution.py:624
  514.0 1.4 fusion.2
  515.4 1.7 slice_reduce_fusion
  517.1 2.5 slice.53
  519.6 0.6 convert_element_type.42
  520.3 0.9 slice.54
  521.1 2.5 fusion.1
  523.6 0.4 slice-done.1
  524.0 4.5 convert.1
  (28 shorter events, 0.1 us)
Async XLA Ops:
  7.2 1.0 copy-start
  7.2 95.8 %all-gather.3.cloned.1.call-start = ((), (), s32[]{:S(2)}) async-start(), calls=%async_computation | async-start | bytes 11354112 | tf_op jit(solution)/shard_map/all_gather | solution.py:688
  11.8 180.7 %all-gather.5.cloned.1.call-start = ((), (), s32[]{:S(2)}) async-start(), calls=%async_computation.1 | async-start | bytes 5898240 | tf_op jit(solution)/shard_map/all_gather | solution.py:697
  13.2 12.8 %copy-start.3 = (f32[1,768]{1,0:T(1,128)}, f32[1,768]{1,0:T(1,128)S(1)}, u32[]{:S(2)}) copy-start(f32[1,768]{1,0:T(1,128)S(1)} %stack.36.gain_ref) | copy-start | bytes 9220
  26.7 76.3 %copy-start.4 = (f32[768]{0:T(1024)S(1)}, f32[768]{0:T(1024)}, u32[]{:S(2)}) copy-start(f32[768]{0:T(1024)} %param.24) | copy-start | bytes 9220
  26.7 76.3 %copy-start.5 = (f32[768]{0:T(1024)S(1)}, f32[768]{0:T(1024)}, u32[]{:S(2)}) copy-start(f32[768]{0:T(1024)} %param.25) | copy-start | bytes 9220
  26.7 76.4 %copy-start.6 = (f32[768]{0:T(1024)S(1)}, f32[768]{0:T(1024)}, u32[]{:S(2)}) copy-start(f32[768]{0:T(1024)} %param.26) | copy-start | bytes 9220
  26.7 76.4 %copy-start.7 = (f32[768]{0:T(1024)S(1)}, f32[768]{0:T(1024)}, u32[]{:S(2)}) copy-start(f32[768]{0:T(1024)} %param.30) | copy-start | bytes 9220
  514.0 5.6 %copy-start.2 = (bf16[8,288,768]{2,1,0:T(8,128)(2,1)S(1)}, bf16[8,288,768]{2,1,0:T(8,128)(2,1)}, u32[]{:S(2)}) copy-start(bf16[8,288,768]{2,1,0:T(8,128)(2,1)} %get-tuple-element.62) | copy-start | bytes 10616836
  520.3 3.4 slice-start
  521.1 2.9 slice-start.1
  524.0 4.5 copy-start.1
Sparse Core Ops, SparseCore 0:
  11.9 90.9 all-gather.2
  104.5 87.9 all-gather.4

commit v2 on v1

--- a/solution.py
+++ b/solution.py
@@ -127,23 +127,27 @@
         acc = acc * jnp.exp2(top - new_top) + mm(values[:, part], powers, NN)
         top = new_top
     total = acc[HEAD_DIM : HEAD_DIM + 1]
-    ctx_ref[...] = (acc[:HEAD_DIM] / total).astype(BF)
+    ctx = (acc[:HEAD_DIM] / total).astype(BF)
+    size = ctx_ref.shape[2]
+    for i in range(ctx_ref.shape[0]):
+        ctx_ref[i] = ctx[:, i * size : (i + 1) * size]
     total_ref[...] = (top + jnp.log2(total))[None]
 
 
-def attend(mask, q, k, v, query_block=3072, block=256):
+def attend(mask, q, k, v, row_block, block=256):
     width, count = q.shape
     heads = width // HEAD_DIM
-    query_block = min(query_block, count)
-    q_spec = pl.BlockSpec((HEAD_DIM, query_block), lambda h, i: (h, i))
-    k_spec = pl.BlockSpec((HEAD_DIM, count), lambda h, i: (h, 0))
+    head_spec = pl.BlockSpec((HEAD_DIM, count), lambda h, i: (h, 0))
     return pl.pallas_call(
         functools.partial(attend_kernel, block=block),
-        grid=(heads, count // query_block),
-        in_specs=[pl.BlockSpec((1, count), lambda h, i: (0, 0)), q_spec, k_spec, k_spec],
-        out_specs=[q_spec, pl.BlockSpec((1, 1, query_block), lambda h, i: (h, 0, i))],
+        grid=(heads, 1),
+        in_specs=[pl.BlockSpec((1, count), lambda h, i: (0, 0)), head_spec, head_spec, head_spec],
+        out_specs=[
+            pl.BlockSpec((count // row_block, HEAD_DIM, row_block), lambda h, i: (0, h, 0)),
+            pl.BlockSpec((1, 1, count), lambda h, i: (h, 0, 0)),
+        ],
         out_shape=[
-            jax.ShapeDtypeStruct((width, count), BF),
+            jax.ShapeDtypeStruct((count // row_block, width, row_block), BF),
             jax.ShapeDtypeStruct((heads, 1, count), F32),
         ],
         scratch_shapes=[pltpu.VMEM((count, 256), BF), pltpu.VMEM((HEAD_DIM + 16, count), BF)],
@@ -153,7 +157,7 @@
 
 
 def attend_back_kernel(
-    mask_ref, q_ref, k_ref, v_ref, ctx_ref, g_ref, total_ref,
+    mask_ref, q_ref, k_ref, v_ref, g_ref, total_ref, dots_ref,
     dq_ref, dk_ref, dv_ref, keys, values, dk_acc, dv_acc, *, block,
 ):
     count = k_ref.shape[1]
@@ -171,11 +175,10 @@
     q = q_ref[...]
     g = g_ref[...]
     high, low = scaled_query(q)
-    dots = jnp.sum(g.astype(F32) * ctx_ref[...].astype(F32), axis=0, keepdims=True)
     query = jnp.concatenate(
         [high, low, jnp.ones((16, width), BF), row_terms(-total_ref[0], 112, width)], axis=0
     )
-    grads = jnp.concatenate([g, row_terms(-dots, HEAD_DIM, width)], axis=0)
+    grads = jnp.concatenate([g, row_terms(-dots_ref[0], HEAD_DIM, width)], axis=0)
     dq = jnp.zeros((HEAD_DIM, width), F32)
     for j in range(count // block):
         part = pl.ds(j * block, block)
@@ -193,7 +196,7 @@
         dv_ref[...] = dv_acc[...].astype(BF)
 
 
-def attend_back(mask, q, k, v, ctx, g, totals, query_block=1024, block=256):
+def attend_back(mask, q, k, v, g, totals, dots, query_block=1024, block=256):
     width, count = q.shape
     heads = width // HEAD_DIM
     q_spec = pl.BlockSpec((HEAD_DIM, query_block), lambda h, i: (h, i))
@@ -202,7 +205,8 @@
         functools.partial(attend_back_kernel, block=block),
         grid=(heads, count // query_block),
         in_specs=[
-            pl.BlockSpec((1, count), lambda h, i: (0, 0)), q_spec, k_spec, k_spec, q_spec, q_spec,
+            pl.BlockSpec((1, count), lambda h, i: (0, 0)), q_spec, k_spec, k_spec, q_spec,
+            pl.BlockSpec((1, 1, query_block), lambda h, i: (h, 0, i)),
             pl.BlockSpec((1, 1, query_block), lambda h, i: (h, 0, i)),
         ],
         out_specs=[q_spec, k_spec, k_spec],
@@ -215,19 +219,72 @@
         ],
         compiler_params=pltpu.CompilerParams(vmem_limit_bytes=VMEM_LIMIT),
         name="attend_back",
-    )(mask, q, k, v, ctx, g, totals)
+    )(mask, q, k, v, g, totals, dots)
+
+
+def to_peer(j, source, target, send_sem, recv_sem):
+    parts = lax.axis_size("mp")
+    return pltpu.make_async_remote_copy(
+        src_ref=source, dst_ref=target, send_sem=send_sem, recv_sem=recv_sem,
+        device_id={"mp": lax.rem(lax.axis_index("mp") + j, parts)}, device_id_type=MESH,
+    )
+
+
+def meet_group():
+    parts = lax.axis_size("mp")
+    barrier = pltpu.get_barrier_semaphore()
+    for j in range(1, parts):
+        pl.semaphore_signal(
+            barrier, inc=1, device_id={"mp": lax.rem(lax.axis_index("mp") + j, parts)},
+            device_id_type=MESH,
+        )
+    pl.semaphore_wait(barrier, parts - 1)
+
+
+def block_copy(own_ref, all_ref, send, recv, j, b, slot, source):
+    return to_peer(j, own_ref.at[b], all_ref.at[slot, source], send.at[slot, j], recv.at[slot, source])
+
+
+def spread_kernel(own_ref, all_ref, send, recv):
+    me, parts = lax.axis_index("mp"), lax.axis_size("mp")
+    meet_group()
+    for b in range(all_ref.shape[0]):
+        for j in range(1, parts):
+            block_copy(own_ref, all_ref, send, recv, j, b, b, me).start()
+    for b in range(all_ref.shape[0]):
+        all_ref[b, me] = own_ref[b]
+    for b in range(all_ref.shape[0]):
+        for j in range(1, parts):
+            source = lax.rem(me - j + parts, parts)
+            block_copy(own_ref, all_ref, send, recv, j, b, b, source).wait()
+
+
+def spread(ctx, parts, ahead):
+    full = pl.BlockSpec(memory_space=pltpu.VMEM)
+    return pl.pallas_call(
+        spread_kernel,
+        in_specs=[full],
+        out_specs=full,
+        out_shape=jax.ShapeDtypeStruct((ahead, parts, *ctx.shape[1:]), BF),
+        scratch_shapes=[pltpu.SemaphoreType.DMA((ahead, parts))] * 2,
+        compiler_params=pltpu.CompilerParams(
+            vmem_limit_bytes=VMEM_LIMIT, collective_id=1, has_side_effects=True
+        ),
+        name="spread",
+    )(ctx)
 
 
 def middle_kernel(
-    count_ref, ctx_ref, in_ref, grad_ref, w_ref, vec_ref,
-    out_ref, mixed_grad_ref, ctx_grad_ref, low_sums_ref, rows_ref, sums_ref, outer_ref,
-    *, parts, hidden, width,
+    count_ref, ahead_ref, own_ref, in_ref, grad_ref, w_ref, vec_ref,
+    out_ref, mixed_grad_ref, ctx_grad_ref, dots_ref, low_sums_ref, rows_ref,
+    sums_ref, outer_ref, ctx_ref, landed_ref, send, recv, *, parts, hidden, width,
 ):
     me = lax.axis_index("mp")
     step = pl.program_id(0)
     block, features = in_ref.shape
     down, outer, tail = features, features + hidden, features + hidden + width
     pieces = w_ref.shape[1]
+    ahead = ahead_ref.shape[0]
 
     def shard(s, start, size):
         low = start // pieces
@@ -240,6 +297,24 @@
         rows_ref[...] = jnp.zeros_like(rows_ref)
         for s in range(parts):
             outer_ref[s * width : (s + 1) * width, :] = shard(s, outer, width)
+        meet_group()
+        for slot in range(landed_ref.shape[0]):
+            for j in range(1, parts):
+                block_copy(own_ref, landed_ref, send, recv, j, slot + ahead, slot, me).start()
+
+    @pl.when(step < ahead)
+    def _():
+        for s in range(parts):
+            ctx_ref[s * width : (s + 1) * width, :] = ahead_ref[step, s]
+
+    @pl.when(step >= ahead)
+    def _():
+        for j in range(1, parts):
+            source = lax.rem(me - j + parts, parts)
+            block_copy(own_ref, landed_ref, send, recv, j, step, step - ahead, source).wait()
+        landed_ref[step - ahead, me] = own_ref[step]
+        for s in range(parts):
+            ctx_ref[s * width : (s + 1) * width, :] = landed_ref[step - ahead, s]
 
     mixed = in_ref[...].astype(F32) + vec_ref[0:1] + mm(ctx_ref[...], outer_ref[...], TN)
     n, inverse = normed(mixed)
@@ -273,7 +348,11 @@
     mixed_grad_ref[...] = grad_mixed
     mixed_low = grad_mixed.astype(BF)
     own = pl.ds(me * width, width)
-    ctx_grad_ref[...] = mm(outer_ref[own, :], mixed_low, NT).astype(BF)
+    ctx_grad = mm(outer_ref[own, :], mixed_low, NT).astype(BF)
+    ctx_grad_ref[...] = ctx_grad
+    products = ctx_grad.astype(F32) * ctx_ref[own, :].astype(F32)
+    for h in range(width // HEAD_DIM):
+        dots_ref[h] = jnp.sum(products[h * HEAD_DIM : (h + 1) * HEAD_DIM], axis=0, keepdims=True)
     sums_ref[outer : outer + width, :] += mm(
         ctx_ref[own, :], mixed_low, NN
     )
@@ -293,9 +372,11 @@
         low_sums_ref[tail:] = jnp.zeros((low_sums_ref.shape[0] - tail, features), BF)
 
 
-def middle(counts, ctx, rows, grads, weights, vectors, hidden, width, held, block=512):
+def middle(counts, ahead, ctx, rows, grads, weights, vectors, hidden, width, held):
     count, features = rows.shape
     parts = weights.shape[0]
+    block = ctx.shape[2]
+    rest = ctx.shape[0] - ahead.shape[0]
     row_spec = pl.BlockSpec((block, features), lambda i: (i, 0))
     sums = features + hidden + width
     return pl.pallas_call(
@@ -303,7 +384,8 @@
         grid=(count // block,),
         in_specs=[
             pl.BlockSpec(memory_space=pltpu.SMEM),
-            pl.BlockSpec((parts * width, block), lambda i: (0, i)),
+            pl.BlockSpec(ahead.shape, lambda i: (0, 0, 0, 0), pipeline_mode=pl.Buffered(1)),
+            pl.BlockSpec(ctx.shape, lambda i: (0, 0, 0), pipeline_mode=pl.Buffered(1)),
             row_spec,
             row_spec,
             pl.BlockSpec(weights.shape, lambda i: (0, 0, 0, 0), pipeline_mode=pl.Buffered(1)),
@@ -313,6 +395,7 @@
             row_spec,
             row_spec,
             pl.BlockSpec((width, block), lambda i: (0, i)),
+            pl.BlockSpec((width // HEAD_DIM, 1, block), lambda i: (0, 0, i)),
             pl.BlockSpec((held, features), lambda i: (0, 0), pipeline_mode=pl.Buffered(1)),
             pl.BlockSpec((8, features), lambda i: (0, 0)),
         ],
@@ -320,15 +403,23 @@
             jax.ShapeDtypeStruct((count, features), BF),
             jax.ShapeDtypeStruct((count, features), F32),
             jax.ShapeDtypeStruct((width, count), BF),
+            jax.ShapeDtypeStruct((width // HEAD_DIM, 1, count), F32),
             jax.ShapeDtypeStruct((held, features), BF),
             jax.ShapeDtypeStruct((8, features), F32),
         ],
         scratch_shapes=[
-            pltpu.VMEM((sums, features), F32), pltpu.VMEM((parts * width, features), BF)
-        ],
-        compiler_params=pltpu.CompilerParams(vmem_limit_bytes=VMEM_LIMIT),
+            pltpu.VMEM((sums, features), F32),
+            pltpu.VMEM((parts * width, features), BF),
+            pltpu.VMEM((parts * width, block), BF),
+            pltpu.VMEM((rest, parts, width, block), BF),
+            pltpu.SemaphoreType.DMA((rest, parts)),
+            pltpu.SemaphoreType.DMA((rest, parts)),
+        ],
+        compiler_params=pltpu.CompilerParams(
+            vmem_limit_bytes=VMEM_LIMIT, collective_id=2, has_side_effects=True
+        ),
         name="middle",
-    )(counts, ctx, rows, grads, weights, vectors)
+    )(counts, ahead, ctx, rows, grads, weights, vectors)
 
 
 def project_back_kernel(
@@ -692,16 +783,16 @@
     bias = jnp.concatenate([query_bias, jnp.zeros_like(query_bias), value_bias])[:, None]
     first, q, k, v = front(rows, weight, bias, jnp.stack([first_gain, first_bias]))
     mask = jnp.where(jnp.arange(slots)[None, :] < counts[:, None], 0.0, -1e30).astype(F32)
-    ctx, totals = attend(mask, q, k, v)
-    ctx, weights = lax.optimization_barrier((ctx, weights))
-    all_ctx = lax.all_gather(ctx, "mp", axis=0, tiled=True)
+    row_block = 512
+    ctx, totals = attend(mask, q, k, v, row_block)
+    ahead = spread(ctx, parts, slots // row_block // 3)
     vectors = jnp.stack([out_bias, second_gain, second_bias, down_bias])
     used = features + hidden + 4 * width
     held = -(-used // (16 * copies)) * 16 * copies
-    outputs, grad_mixed, ctx_grad, sums, small = middle(
-        counts, all_ctx, rows, grads, weights, vectors, hidden, width, held
-    )
-    dq, dk, dv = attend_back(mask, q, k, v, ctx, ctx_grad, totals)
+    outputs, grad_mixed, ctx_grad, dots, sums, small = middle(
+        counts, ahead, ctx, rows, grads, weights, vectors, hidden, width, held
+    )
+    dq, dk, dv = attend_back(mask, q, k, v, ctx_grad, totals, dots)
     late = features + hidden + width
     partial, vec, sums = project_back(first, rows, dq, dk, dv, weight, small, sums, late)
     chunks = next(c for c in (16, 8, 4, 2, 1) if slots % (8 * parts * c) == 0)

time: 540 us -> 494 us (0.915)
  waiting for transfers between devices: 131 us -> 2.54 us
  Pallas kernels: 365 us -> 443 us
    all_gather x1 -> x0, waiting for transfers between devices: 88.8 us -> none  [per_device(): all_ctx = lax.all_gather(ctx, 'mp', axis=0, tiled=True)]
    pallas_call x0 -> x1, Pallas kernels: none -> 65.1 us  [spread(): pl.pallas_call(spread_kernel, in_specs=[full], out_specs=full, out_shape=...]
    all_gather x1, waiting for transfers between devices: 42.2 us -> 2.52 us  [per_device(): weights = lax.all_gather(piece, ('mp', 'dp'), axis=0, tiled=True)]
    pallas_call x1, Pallas kernels: 134 us -> 141 us  [finish(): pl.pallas_call(functools.partial(finish_kernel, parts=parts, copies=copie...]
    pallas_call x1, Pallas kernels: 103 us -> 109 us  [middle(): pl.pallas_call(functools.partial(middle_kernel, parts=parts, hidden=hidde...]
  transfers between devices with their start and end apart: 2 -> 1, of which waited for: 2 -> 1; matrix products, arithmetic and copies ran while one was open for 1% -> 2% of each run, Pallas kernels for 8% -> 22%
where the time goes in v2:
time: 494 us; the launch traced here: 489 us
  Pallas kernels  443 us (90%)
  local copies, waits for them, and re-layouts  20.3 us (4%)
  between operations  15.2 us (3%)
  other arithmetic  8.49 us (2%)
    pallas_call x1, Pallas kernels, finish(): pl.pallas_call(functools.partial(finish_kernel, parts=parts, copies=copie...  141 us
    pallas_call x1, Pallas kernels, middle(): pl.pallas_call(functools.partial(middle_kernel, parts=parts, hidden=hidde...  109 us
    pallas_call x1, Pallas kernels, attend_back(): pl.pallas_call(functools.partial(attend_back_kernel, block=block), grid=(...  70.2 us
    pallas_call x1, Pallas kernels, spread(): pl.pallas_call(spread_kernel, in_specs=[full], out_specs=full, out_shape=...  65.1 us
    pallas_call x1, Pallas kernels, attend(): pl.pallas_call(functools.partial(attend_kernel, block=block), grid=(heads...  34.1 us
    pallas_call x1, Pallas kernels, project_back(): pl.pallas_call(functools.partial(project_back_kernel, width=width, start=...  13.9 us
    pallas_call x1, Pallas kernels, front(): pl.pallas_call(functools.partial(front_kernel, width=width), grid=(count...  9.91 us
  transfers between devices with their start and end apart: 1, of which 1 were waited for; matrix products, arithmetic and copies ran while one was open for 2% of the time, Pallas kernels for 22%

profile of v2, /device:TPU:0, one launch (start us, length us, event | category | flops | bytes accessed | tf_op | source)
XLA Modules:
  0.0 489.2 jit_solution(2763361754612037603)
XLA Ops:
  7.2 0.8 subtract_convert_fusion
  8.1 0.1 copy-done
  8.2 1.0 constant_dynamic-slice_fusion.1
  9.2 2.6 concatenate.6
  12.5 0.7 stack.36.gain_ref
  13.2 0.7 stack.37
  13.9 0.7 stack.39
  14.5 0.7 stack.40
  15.2 0.7 stack.41
  15.9 0.7 stack.42
  16.6 0.8 pad_maximum_fusion.2
  17.4 0.9 broadcast_in_dim.25.bias_ref
  18.2 0.6 pad_maximum_fusion.1.gain_ref
  18.8 9.9 %front.1 = (bf16[3072,768]{1,0:T(8,128)(2,1)}, bf16[192,3072]{1,0:T(8,128)(2,1)}, bf16[192,3072]{1,0:T(8,128)(2,1)}, bf16[192,3072]{1,0:T(8,128)(2,1)}) custom-call(bf16[3072,768]{1,0:T(8,128)(2,1)} %bitcast.21, bf16[576,768]{1,0:T(8,128)(2,1)} %bitcast.38, f32[576,1]{1,0:T(8,128)} %broadcast_in_dim.25.bias_ref, f32[2,768]{1,0:T(2,128)} %pad_maximum_fusion.1.gain_ref), custom_call_target="tpu_custom_call" | custom-call | tf_op jit(solution)/shard_map/front/pallas_call | solution.py:71
  28.7 0.6 compare_select_fusion.mask_ref
  29.4 34.1 %attend.1 = (bf16[6,192,512]{2,1,0:T(8,128)(2,1)}, f32[3,1,3072]{2,1,0:T(1,128)}) custom-call(f32[1,3072]{1,0:T(1,128)} %compare_select_fusion.mask_ref, bf16[192,3072]{1,0:T(8,128)(2,1)} %get-tuple-element.39.q_ref, bf16[192,3072]{1,0:T(8,128)(2,1)} %get-tuple-element.40.k_ref, bf16[192,3072]{1,0:T(8,128)(2,1)} %get-tuple-element.41.v_ref), custom_call_target="tpu_custom_call" | custom-call | tf_op jit(solution)/shard_map/attend/pallas_call | solution.py:141
  63.4 65.1 %spread.1.ahead_ref = bf16[2,4,192,512]{3,2,1,0:T(8,128)(2,1)} custom-call(bf16[6,192,512]{2,1,0:T(8,128)(2,1)} %get-tuple-element.42.own_ref), custom_call_target="tpu_custom_call" | custom-call | tf_op jit(solution)/shard_map/spread/pallas_call | solution.py:264
  128.5 0.6 pad_maximum_fusion.vec_ref
  129.1 2.5 all-gather.2.cloned.1.call-done
  131.7 108.5 %middle.1 = (bf16[3072,768]{1,0:T(8,128)(2,1)}, f32[3072,768]{1,0:T(8,128)}, bf16[192,3072]{1,0:T(8,128)(2,1)}, f32[3,1,3072]{2,1,0:T(1,128)}, bf16[2304,768]{1,0:T(8,128)(2,1)}, /*index=5*/f32[8,768]{1,0:T(8,128)}) custom-call(s32[1]{0:T(128)} %copy.35.count_ref, bf16[2,4,192,512]{3,2,1,0:T(8,128)(2,1)} %spread.1.ahead_ref, ...), custom_call_target="tpu_custom_call" | custom-call | tf_op jit(solution)/shard_map/middle/pallas_call | solution.py:382
  240.2 70.2 %attend_back.1 = (bf16[192,3072]{1,0:T(8,128)(2,1)}, bf16[192,3072]{1,0:T(8,128)(2,1)}, bf16[192,3072]{1,0:T(8,128)(2,1)}) custom-call(f32[1,3072]{1,0:T(1,128)} %compare_select_fusion.mask_ref, bf16[192,3072]{1,0:T(8,128)(2,1)} %get-tuple-element.39.q_ref, bf16[192,3072]{1,0:T(8,128)(2,1)} %get-tuple-element.40.k_ref, ...), custom_call_target="tpu_custom_call" | custom-call | tf_op jit(solution)/shard_map/attend_back/pallas_call | solution.py:204
  310.4 13.9 %project_back.1 = (bf16[3072,768]{1,0:T(8,128)(2,1)}, f32[24,768]{1,0:T(8,128)}, bf16[2304,768]{1,0:T(8,128)(2,1)}) custom-call(bf16[3072,768]{1,0:T(8,128)(2,1)} %get-tuple-element.45.first_ref, bf16[3072,768]{1,0:T(8,128)(2,1)} %bitcast.23, bf16[192,3072]{1,0:T(8,128)(2,1)} %get-tuple-element.49.dq_ref, ...), custom_call_target="tpu_custom_call", output_to_operand_aliasing={{2}: (7, {})} | custom-call | tf_op jit(solution)/shard_map/project_back/pallas_call | solution.py:462
  324.4 140.8 %finish.1 = (bf16[4,16,48,768]{3,2,1,0:T(8,128)(2,1)}, f32[24,768]{1,0:T(8,128)}, bf16[8,288,768]{2,1,0:T(8,128)(2,1)}) custom-call(bf16[4,16,48,768]{3,2,1,0:T(8,128)(2,1)} %bitcast.37, bf16[4,16,48,768]{3,2,1,0:T(8,128)(2,1)} %bitcast.24, f32[4,16,48,768]{3,2,1,0:T(8,128)} %bitcast.29, f32[1,768]{1,0:T(1,128)} %copy-done.3, ...), custom_call_target="tpu_custom_call" | custom-call | tf_op jit(solution)/shard_map/finish/pallas_call | solution.py:715
  465.2 1.4 fusion.2
  466.6 1.7 slice_reduce_fusion
  468.3 2.5 slice.53
  470.8 0.6 convert_element_type.42
  471.5 0.9 slice.54
  472.3 2.5 fusion.1
  474.8 0.4 slice-done.1
  475.2 4.5 convert.1
  479.7 2.2 copy.36
  (24 shorter events, 0.1 us)
Async XLA Ops:
  7.2 1.0 copy-start
  7.2 124.5 %all-gather.2.cloned.1.call-start = ((), (), s32[]{:S(2)}) async-start(), calls=%async_computation | async-start | bytes 11354112 | tf_op jit(solution)/shard_map/all_gather | solution.py:779
  13.2 15.6 %copy-start.3 = (f32[1,768]{1,0:T(1,128)}, f32[1,768]{1,0:T(1,128)S(1)}, u32[]{:S(2)}) copy-start(f32[1,768]{1,0:T(1,128)S(1)} %stack.36.gain_ref) | copy-start | bytes 9220
  465.2 5.6 %copy-start.2 = (bf16[8,288,768]{2,1,0:T(8,128)(2,1)S(1)}, bf16[8,288,768]{2,1,0:T(8,128)(2,1)}, u32[]{:S(2)}) copy-start(bf16[8,288,768]{2,1,0:T(8,128)(2,1)} %get-tuple-element.60) | copy-start | bytes 10616836
  471.5 3.4 slice-start
  472.3 2.9 slice-start.1
  474.8 4.9 slice-start.2
  475.2 4.5 slice-start.3
  479.7 2.2 copy-start.1
Sparse Core Ops, SparseCore 0:
  11.9 119.6 all-gather.1
